TPU v7x, 512 devices: a whole 4x4x16 slice. The times are simulated.
512 devices in a mesh: row: 16 (over y, x), col: 32 (over z, core).
Axes of the slice: x: 4, y: 4, z: 16, core: 2. Of those that a mesh axis runs over, the one named last changes fastest.
Arguments:
- tokens: bfloat16 [4096, 8192], P('row', 'col'), may hold values from -6 to 6
- w_in: bfloat16 [8192, 3, 8192], P('row', None, 'col'), may hold values from -0.0625 to 0.0625
- filt_in: float32 [7, 3, 8192], P(None, None, 'col'), may hold values from -2.4 to 2.4
- filt_mix: float32 [7, 8192], P(None, 'col'), may hold values from -2.4 to 2.4
Outputs:
- gated: bfloat16 [4096, 8192], P('row', 'col')
All inputs are finite; a program needn't handle non-finite values.
Results may differ from a plain program's by a relative error of at most 0.0064.
Values may be sent and summed in bfloat16 or wider, within the bound.
A program may use at most 64 MiB of HBM per device.

v0:
```python
import jax
import jax.numpy as jnp
from jax import lax
from jax.sharding import PartitionSpec as P


def passed_along(block, axis, distance):
    devices = range(lax.axis_size(axis))
    route = [(i - distance, i) for i in devices if i - distance in devices]
    return lax.ppermute(block, axis, route)


def taps(ext, filt, count):
    total = filt[0] * ext[6 : 6 + count]
    for shift_s in range(1, 7):
        total = total + filt[shift_s] * ext[6 - shift_s : 6 - shift_s + count]
    return total


def per_device(tokens, w_in, filt_in, filt_mix):
    rows = tokens.shape[0]
    cols = w_in.shape[2]
    strip = lax.all_gather(tokens, "col", axis=1, tiled=True)
    piece = lax.all_gather(w_in, "row", axis=0, tiled=True)
    flat_piece = piece.reshape(piece.shape[0], 3 * cols)
    summed = jnp.dot(strip, flat_piece, preferred_element_type=jnp.float32)
    proj = summed.astype(jnp.bfloat16).reshape(rows, 3, cols)
    starts_seq = lax.axis_index("row") == 0
    keep_f = jnp.where(starts_seq, 0.0, 1.0).astype(jnp.float32)
    rim = passed_along(proj[rows - 6 :], "row", 1)
    ext = jnp.concatenate([rim.astype(jnp.float32) * keep_f, proj.astype(jnp.float32)], axis=0)
    conv = taps(ext, filt_in, rows)
    prod = conv[:, 1] * conv[:, 2]
    prod_rim = passed_along(prod[rows - 6 :], "row", 1)
    ext_prod = jnp.concatenate([prod_rim * keep_f, prod], axis=0)
    mix = taps(ext_prod, filt_mix, rows)
    query = conv[:, 0]
    return (query * mix).astype(jnp.bfloat16)


def solution(mesh):
    return jax.shard_map(
        per_device,
        mesh=mesh,
        in_specs=(P("row", "col"), P("row", None, "col"), P(None, None, "col"), P(None, "col")),
        out_specs=P("row", "col"),
        check_vma=False,
    )
```

profile of v0, /device:TPU:8, one launch (start us, length us, event | category | flops | bytes accessed | tf_op | source)
XLA Modules:
  0.0 247.7 jit_solution(13775816980189097958)
XLA Ops:
  6.5 0.0 all-gather.3.cloned.1.call-start
  6.5 0.7 all-gather.3.cloned.1.call-update
  7.3 0.0 all-gather.5.cloned.1.call-start
  7.3 2.3 copy.8
  9.6 0.0 all-gather.5.cloned.1.call-update
  9.6 1.0 fusion.36
  10.7 83.2 %all-gather.3.cloned.1.call-done = bf16[256,8192]{1,0:T(8,128)(2,1)} async-done(((bf16[256,256]{1,0:T(8,128)(2,1)}), bf16[256,8192]{1,0:T(8,128)(2,1)}) %all-gather.3.cloned.1.call-update) | async-done | bytes 4194320 | tf_op jit(solution)/shard_map/all_gather | solution.py:23
  93.9 114.1 %all-gather.5.cloned.1.call-done = bf16[8192,3,256]{0,2,1:T(8,128)(2,1)} async-done(((bf16[512,3,256]{0,2,1:T(8,128)(2,1)}), bf16[8192,3,256]{0,2,1:T(8,128)(2,1)}) %all-gather.5.cloned.1.call-update) | async-done | bytes 12582928 | tf_op jit(solution)/shard_map/all_gather | solution.py:24
  208.0 0.0 copy-start
  208.0 9.3 %convolution_convert_fusion = bf16[256,768]{1,0:T(8,128)(2,1)S(1)} fusion(bf16[256,8192]{1,0:T(8,128)(2,1)} %all-gather.3.cloned.1.call-done, bf16[8192,768]{0,1:T(8,128)(2,1)} %bitcast.45), kind=kOutput, calls=%fused_computation.10 | convolution fusion | flops 3221422080 | bytes 17170432 | tf_op jit(solution)/shard_map/dot_general | solution.py:26
  217.3 0.2 copy.12
  217.5 2.2 collective-permute-start
  219.7 0.0 copy-done
  219.8 0.2 copy.9
  219.9 7.3 %collective-permute-done = bf16[6,3,256]{0,2,1:T(8,128)(2,1)S(1)} collective-permute-done((bf16[6,3,256]{0,2,1:T(8,128)(2,1)S(1)}, bf16[6,3,256]{0,2,1:T(8,128)(2,1)S(1)}, u32[]{:S(2)}, u32[]{:S(2)}) %collective-permute-start) | collective-permute-done | bytes 9248 | tf_op jit(solution)/shard_map/ppermute | solution.py:10
  227.3 2.7 %fusion.3 = f32[256,3,256]{0,2,1:T(8,128)S(1)} fusion(f32[256,3,256]{0,2,1:T(8,128)S(1)} %bitcast.35, f32[6,3,256]{0,2,1:T(8,128)S(1)} %convert_multiply_fusion, f32[3,256]{1,0:T(4,128)S(1)} %get-tuple-element.19, f32[3,256]{1,0:T(4,128)S(1)} %get-tuple-element.20, f32[3,256]{1,0:T(4,128)S(1)} %get-tuple-element.21, f32[3,256]{1,0:T(4,128)S(1)} %get-tuple-element.22, ...), kind=kLoop, calls=%fused_computation.19 | loop fusion | flops 3735552 | bytes 1612800 | tf_op jit(solution)/shard_map/add | solution.py:16
  230.1 0.1 slice_bitcast_fusion.1
  230.2 1.9 collective-permute-start.1
  232.1 7.0 %collective-permute-done.1 = f32[6,256]{0,1:T(8,128)S(1)} collective-permute-done((f32[6,256]{0,1:T(8,128)S(1)}, f32[6,256]{0,1:T(8,128)S(1)}, u32[]{:S(2)}, u32[]{:S(2)}) %collective-permute-start.1) | collective-permute-done | bytes 6176 | tf_op jit(solution)/shard_map/ppermute | solution.py:10
  239.2 0.9 fusion.22
  240.1 0.8 copy.11
  (10 shorter events, 0.1 us)
Async XLA Ops:
  6.5 87.4 %all-gather.3.cloned.1.call-start = ((), (), s32[]{:S(2)}) async-start(), calls=%async_computation | async-start | bytes 4325376 | tf_op jit(solution)/shard_map/all_gather | solution.py:23
  7.3 200.7 %all-gather.5.cloned.1.call-start = ((), (), s32[]{:S(2)}) async-start(), calls=%async_computation.1 | async-start | bytes 13369344 | tf_op jit(solution)/shard_map/all_gather | solution.py:24
  208.0 11.7 %copy-start = (f32[7,256]{1,0:T(8,128)S(1)}, f32[7,256]{1,0:T(8,128)}, u32[]{:S(2)}) copy-start(f32[7,256]{1,0:T(8,128)} %param.7) | copy-start | bytes 21508
  217.5 9.8 %collective-permute-start = (bf16[6,3,256]{0,2,1:T(8,128)(2,1)S(1)}, bf16[6,3,256]{0,2,1:T(8,128)(2,1)S(1)}, u32[]{:S(2)}, u32[]{:S(2)}) collective-permute-start(bf16[6,3,256]{0,2,1:T(8,128)(2,1)S(1)} %bitcast.36), channel_id=1, source_target_pairs={{0,32},{32,64},{64,96},{96,128},{128,160},{160,192},{192,224},{224... | collective-permute-start | bytes 27656 | tf_op jit(solution)/shard_map/ppermute | solution.py:10
  230.2 9.0 %collective-permute-start.1 = (f32[6,256]{0,1:T(8,128)S(1)}, f32[6,256]{0,1:T(8,128)S(1)}, u32[]{:S(2)}, u32[]{:S(2)}) collective-permute-start(f32[6,256]{0,1:T(8,128)S(1)} %slice_bitcast_fusion.1), channel_id=1, source_target_pairs={{0,32},{32,64},{64,96},{96,128},{128,160},{160,192},{192,224},{224... | collective-permute-start | bytes 18440 | tf_op jit(solution)/shard_map/ppermute | solution.py:10
Sparse Core Ops, SparseCore 0:
  9.4 84.4 all-gather.2
  96.9 111.0 all-gather.4
where the time goes:
time: 248 us
  waiting for transfers between devices  212 us (85%)
  between operations  13.5 us (5%)
  matrix products  9.31 us (4%)
  local copies, waits for them, and re-layouts  4.56 us (2%)
  starting transfers between devices  4.17 us (2%)
  other arithmetic  3.72 us (2%)
    all_gather x1, waiting for transfers between devices, per_device(): piece = lax.all_gather(w_in, 'row', axis=0, tiled=True)  114 us
    all_gather x1, waiting for transfers between devices, per_device(): strip = lax.all_gather(tokens, 'col', axis=1, tiled=True)  83.2 us
    ppermute x2, waiting for transfers between devices, passed_along(): return lax.ppermute(block, axis, route)  14.3 us
    dot_general x1, matrix products, per_device(): summed = jnp.dot(strip, flat_piece, preferred_element_type=jnp.float32)  9.31 us
  transfers between devices with their start and end apart: 4, of which 4 were waited for; matrix products, arithmetic and copies ran while one was open for 1% of the time, Pallas kernels for 0%

commit v1 on v0

--- a/solution.py
+++ b/solution.py
@@ -20,7 +20,9 @@
 def per_device(tokens, w_in, filt_in, filt_mix):
     rows = tokens.shape[0]
     cols = w_in.shape[2]
-    strip = lax.all_gather(tokens, "col", axis=1, tiled=True)
+    strip = jnp.concatenate(
+        lax.all_to_all(jnp.stack([tokens] * lax.axis_size("col")), "col", 0, 0), axis=1
+    )
     piece = lax.all_gather(w_in, "row", axis=0, tiled=True)
     flat_piece = piece.reshape(piece.shape[0], 3 * cols)
     summed = jnp.dot(strip, flat_piece, preferred_element_type=jnp.float32)

time: 248 us -> 258 us (1.040)
  the two profiles are of different devices: /device:TPU:8 before, /device:TPU:40 now
where the time goes in v1:
time: 258 us
  waiting for transfers between devices  203 us (79%)
  starting transfers between devices  20.9 us (8%)
  between operations  13.6 us (5%)
  matrix products  9.34 us (4%)
  local copies, waits for them, and re-layouts  6.97 us (3%)
  other arithmetic  3.72 us (1%)
    all_to_all x1, waiting for transfers between devices, per_device(): lax.all_to_all(jnp.stack([tokens] * lax.axis_size('col')), 'col', 0, 0)  190 us
    all_to_all x1, starting transfers between devices, per_device(): lax.all_to_all(jnp.stack([tokens] * lax.axis_size('col')), 'col', 0, 0)  15.5 us
    ppermute x2, waiting for transfers between devices, passed_along(): return lax.ppermute(block, axis, route)  13 us
    dot_general x1, matrix products, per_device(): summed = jnp.dot(strip, flat_piece, preferred_element_type=jnp.float32)  9.34 us
    ppermute x2, starting transfers between devices, passed_along(): return lax.ppermute(block, axis, route)  5.32 us
  transfers between devices with their start and end apart: 4, of which 3 were waited for; matrix products, arithmetic and copies ran while one was open for 1% of the time, Pallas kernels for 0%

profile of v1, /device:TPU:40, one launch (start us, length us, event | category | flops | bytes accessed | tf_op | source)
XLA Modules:
  0.0 257.6 jit_solution(8381977825179619971)
XLA Ops:
  6.5 0.0 all-gather.2.cloned.1.call-start
  6.5 2.3 copy.9
  8.8 0.0 all-gather.2.cloned.1.call-update
  8.9 1.0 copy.8
  9.9 2.4 stack.2
  12.3 0.0 copy-start
  12.3 15.5 %all-to-all-start = ((bf16[32,256,256]{1,2,0:T(8,128)(2,1)}), bf16[32,256,256]{1,2,0:T(8,128)(2,1)}, u32[]{:S(2)}, u32[]{:S(2)}) async-start(bf16[32,256,256]{1,2,0:T(8,128)(2,1)} %stack.2), calls=%async_computation | async-start | bytes 8388608 | tf_op jit(solution)/shard_map/all_to_all | solution.py:24
  27.8 0.0 copy-done
  27.9 190.1 %all-to-all-done = bf16[32,256,256]{1,2,0:T(8,128)(2,1)} async-done(((bf16[32,256,256]{1,2,0:T(8,128)(2,1)}), bf16[32,256,256]{1,2,0:T(8,128)(2,1)}, u32[]{:S(2)}, u32[]{:S(2)}) %all-to-all-start) | async-done | bytes 4194336 | tf_op jit(solution)/shard_map/all_to_all | solution.py:24
  218.0 0.0 all-gather.2.cloned.1.call-done
  218.0 0.0 copy-start.1
  218.0 9.3 %convolution_convert_fusion = bf16[256,768]{1,0:T(8,128)(2,1)S(1)} fusion(bf16[256,8192]{0,1:T(8,128)(2,1)} %bitcast.1, bf16[8192,768]{0,1:T(8,128)(2,1)} %bitcast.48), kind=kOutput, calls=%fused_computation.10 | convolution fusion | flops 3221422080 | bytes 17170432 | tf_op jit(solution)/shard_map/dot_general | solution.py:28
  227.4 0.2 copy.13
  227.5 3.4 %collective-permute-start = (bf16[6,3,256]{0,2,1:T(8,128)(2,1)S(1)}, bf16[6,3,256]{0,2,1:T(8,128)(2,1)S(1)}, u32[]{:S(2)}, u32[]{:S(2)}) collective-permute-start(bf16[6,3,256]{0,2,1:T(8,128)(2,1)S(1)} %bitcast.39), channel_id=1, source_target_pairs={{0,32},{32,64},{64,96},{96,128},{128,160},{160,192},{192,224},{224... | collective-permute-start | bytes 27656 | tf_op jit(solution)/shard_map/ppermute | solution.py:10
  230.9 0.0 copy-done.1
  231.0 0.2 copy.10
  231.2 6.0 %collective-permute-done = bf16[6,3,256]{0,2,1:T(8,128)(2,1)S(1)} collective-permute-done((bf16[6,3,256]{0,2,1:T(8,128)(2,1)S(1)}, bf16[6,3,256]{0,2,1:T(8,128)(2,1)S(1)}, u32[]{:S(2)}, u32[]{:S(2)}) %collective-permute-start) | collective-permute-done | bytes 9248 | tf_op jit(solution)/shard_map/ppermute | solution.py:10
  237.2 2.7 %fusion.3 = f32[256,3,256]{0,2,1:T(8,128)S(1)} fusion(f32[256,3,256]{0,2,1:T(8,128)S(1)} %bitcast.38, f32[6,3,256]{0,2,1:T(8,128)S(1)} %convert_multiply_fusion, f32[3,256]{1,0:T(4,128)S(1)} %get-tuple-element.19, f32[3,256]{1,0:T(4,128)S(1)} %get-tuple-element.20, f32[3,256]{1,0:T(4,128)S(1)} %get-tuple-element.21, f32[3,256]{1,0:T(4,128)S(1)} %get-tuple-element.22, ...), kind=kLoop, calls=%fused_computation.19 | loop fusion | flops 3735552 | bytes 1612800 | tf_op jit(solution)/shard_map/add | solution.py:16
  240.0 0.1 slice_bitcast_fusion.1
  240.1 1.9 collective-permute-start.1
  242.1 7.0 %collective-permute-done.1 = f32[6,256]{0,1:T(8,128)S(1)} collective-permute-done((f32[6,256]{0,1:T(8,128)S(1)}, f32[6,256]{0,1:T(8,128)S(1)}, u32[]{:S(2)}, u32[]{:S(2)}) %collective-permute-start.1) | collective-permute-done | bytes 6176 | tf_op jit(solution)/shard_map/ppermute | solution.py:10
  249.1 0.9 fusion.22
  250.0 0.8 copy.12
  (11 shorter events, 0.2 us)
Async XLA Ops:
  6.5 211.5 %all-gather.2.cloned.1.call-start = ((), (), s32[]{:S(2)}) async-start(), calls=%async_computation.1 | async-start | bytes 13369344 | tf_op jit(solution)/shard_map/all_gather | solution.py:26
  12.3 15.6 %copy-start = (f32[7,3,256]{2,0,1:T(8,128)S(1)}, f32[7,3,256]{2,0,1:T(8,128)}, u32[]{:S(2)}) copy-start(f32[7,3,256]{2,0,1:T(8,128)} %param.6) | copy-start | bytes 64516
  12.3 205.7 %all-to-all-start = ((bf16[32,256,256]{1,2,0:T(8,128)(2,1)}), bf16[32,256,256]{1,2,0:T(8,128)(2,1)}, u32[]{:S(2)}, u32[]{:S(2)}) async-start(bf16[32,256,256]{1,2,0:T(8,128)(2,1)} %stack.2), calls=%async_computation | async-start | bytes 8388608 | tf_op jit(solution)/shard_map/all_to_all | solution.py:24
  218.0 13.0 %copy-start.1 = (f32[7,256]{1,0:T(8,128)S(1)}, f32[7,256]{1,0:T(8,128)}, u32[]{:S(2)}) copy-start(f32[7,256]{1,0:T(8,128)} %param.7) | copy-start | bytes 21508
  227.5 9.7 %collective-permute-start = (bf16[6,3,256]{0,2,1:T(8,128)(2,1)S(1)}, bf16[6,3,256]{0,2,1:T(8,128)(2,1)S(1)}, u32[]{:S(2)}, u32[]{:S(2)}) collective-permute-start(bf16[6,3,256]{0,2,1:T(8,128)(2,1)S(1)} %bitcast.39), channel_id=1, source_target_pairs={{0,32},{32,64},{64,96},{96,128},{128,160},{160,192},{192,224},{224... | collective-permute-start | bytes 27656 | tf_op jit(solution)/shard_map/ppermute | solution.py:10
  240.1 9.0 %collective-permute-start.1 = (f32[6,256]{0,1:T(8,128)S(1)}, f32[6,256]{0,1:T(8,128)S(1)}, u32[]{:S(2)}, u32[]{:S(2)}) collective-permute-start(f32[6,256]{0,1:T(8,128)S(1)} %slice_bitcast_fusion.1), channel_id=1, source_target_pairs={{0,32},{32,64},{64,96},{96,128},{128,160},{160,192},{192,224},{224... | collective-permute-start | bytes 18440 | tf_op jit(solution)/shard_map/ppermute | solution.py:10
Sparse Core Ops, SparseCore 0:
  10.3 118.6 all-gather.1
